TPU v7x, 256 devices: a whole 4x4x8 slice. The times are simulated.
256 devices in a mesh: sa: 2 (over y_lo), gx: 16 (over z, core), gy: 8 (over x, y_hi).
Axes of the slice: x: 4, y: 4 (y_hi: 2, y_lo: 2; y = y_hi * 2 + y_lo), z: 8, core: 2. Of those that a mesh axis runs over, the one named last changes fastest.
Arguments:
- pred_frames: float32 [12, 32768], P(None, ('sa', 'gx', 'gy')), parts along dimension 1, may hold values from -52 to 52, as said below
- true_frames: float32 [12, 32768], P(None, ('sa', 'gx', 'gy')), parts along dimension 1, may hold values from -52 to 52, as said below
- pred_atoms: float32 [3, 57344], P(None, ('sa', 'gx', 'gy')), parts along dimension 1, may hold values from -52 to 52
- true_atoms: float32 [3, 57344], P(None, ('sa', 'gx', 'gy')), parts along dimension 1, may hold values from -52 to 52
- atom_mask: int32 [57344], P(('sa', 'gx', 'gy')), parts along dimension 0, may hold values from 0 to 1, as said below
- residue_types: int32 [4096], P(('sa', 'gx', 'gy')), parts along dimension 0, may hold values from 0 to 19
- swap_flags: int32 [4096], P(('sa', 'gx', 'gy')), parts along dimension 0, may hold values from 0 to 1
Outputs:
- frame_loss: float32 [32768], P(('sa', 'gx', 'gy')), parts along dimension 0
- atom_loss: float32 [57344], P(('sa', 'gx', 'gy')), parts along dimension 0
- total_loss: float32 [2], P('sa'), parts along dimension 0
There are 2 independent parts, one for each index of `sa`. A program takes and returns all parts, laid end to end along the dimension named above; each array names one. Nothing has to cross between parts.
Inputs may be any that keep to these rules, and one draw needn't show every extreme that they name: `atom_mask`: atom slots 0 to 3 of every residue, its backbone atoms, are 1. `pred_frames`: rows 0 to 8 of each frame hold a rotation matrix, row-major; rows 9 to 11 its translation. `true_frames`: rows 0 to 8 of each frame hold a rotation matrix, row-major; rows 9 to 11 its translation.
All inputs are finite; a program needn't handle non-finite values.
Results may differ from a plain program's by a relative error of at most 0.0001.
Values sent between devices are 32-bit elements; how exact they have to be, the bound alone decides.
A program may use at most 64 MiB of HBM per device.

v0:
```python
import functools
import math
import jax
import jax.numpy as jnp
import numpy as np
from jax import lax
from jax.sharding import Mesh
from jax.sharding import PartitionSpec as P

GY = ("gy_0", "gy_1")
GX = ("gx_0", "gx_1")
GX_GY = ("gx_0", "gx_1", "gy_0", "gy_1")
SA_GX_GY = ("sa", "gx_0", "gx_1", "gy_0", "gy_1")
eps_square = 0.0001
clamp_length = 10.0


def side_by_side(arrays, axis, dim, along):
    widths = [a.shape[along] for a in arrays]
    both = jnp.concatenate(arrays, axis=along)
    result = lax.all_gather(both, axis, axis=dim, tiled=True)
    return tuple(jnp.split(result, [sum(widths[:k]) for k in range(1, len(widths))], axis=along))


def gather_turned(arrays, axis, dims):
    turned = [jnp.moveaxis(a, dim, 0) for a, dim in zip(arrays, dims)]
    both = jnp.concatenate([t.reshape(len(t), -1) for t in turned], axis=1)
    result, at, gathered = (lax.all_gather(both, axis, axis=0, tiled=True), 0, [])
    for t, dim in zip(turned, dims):
        piece = result[:, at : at + t[0].size].reshape(-1, *t.shape[1:])
        gathered.append(jnp.moveaxis(piece, 0, dim))
        at += t[0].size
    return tuple(gathered)


def split_up(value, dim, length):
    lengths = value.shape
    tiles = value.reshape(*lengths[:dim], length, lengths[dim] // length, *lengths[dim + 1 :])
    return jnp.moveaxis(tiles, dim, 0)


def sent_and_summed(value, axis, dim):
    tiles = split_up(value, dim, lax.axis_size(axis))
    arrived = lax.all_to_all(tiles, axis, split_axis=0, concat_axis=0, tiled=True)
    return arrived.sum(axis=0)


def by_axis(value, axes):
    return functools.reduce(lax.psum, axes, value)


def residue_tables():
    atom_counts = np.array([5, 11, 8, 8, 6, 9, 9, 4, 10, 8, 8, 9, 8, 11, 7, 6, 7, 14, 12, 7])
    chi_counts = np.array([0, 4, 2, 2, 1, 3, 3, 0, 2, 2, 2, 4, 3, 2, 2, 1, 1, 2, 2, 1])
    atom_table = (np.arange(14)[None, :] < atom_counts[:, None]).astype(np.float32)
    slot_ids = np.arange(8)[None, :]
    frame_table = (
        (slot_ids == 0) | (slot_ids == 3) | (slot_ids >= 4) & (slot_ids - 3 <= chi_counts[:, None])
    ).astype(np.float32)
    partner_table = np.tile(np.arange(14), (20, 1))
    for restype, swap_pairs in (
        (3, ((6, 7),)),
        (6, ((7, 8),)),
        (13, ((6, 7), (8, 9))),
        (18, ((6, 7), (8, 9))),
    ):
        for first_slot, second_slot in swap_pairs:
            partner_table[restype, first_slot] = second_slot
            partner_table[restype, second_slot] = first_slot
    flip_table = np.zeros((20, 8), np.float32)
    flip_table[3, 5] = 1.0
    flip_table[13, 5] = 1.0
    flip_table[18, 5] = 1.0
    flip_table[6, 6] = 1.0
    sign_table = np.array([1, -1, -1, 1, -1, -1, 1, -1, -1, 1, 1, 1], np.float32)
    return (atom_table, frame_table, partner_table, flip_table, sign_table)


def type_onehot(residue_types):
    return residue_types[:, None] == jnp.arange(20, dtype=jnp.int32)[None, :]


def frame_terms(pred_frames, true_frames, residue_types, swap_flags):
    tables = residue_tables()
    onehot = type_onehot(residue_types).astype(jnp.float32)
    frame_table = jnp.asarray(tables[1], dtype=jnp.float32)
    flip_table = jnp.asarray(tables[3], dtype=jnp.float32)
    sign_table = jnp.asarray(tables[4], dtype=jnp.float32)
    exists = jnp.sum(onehot[:, :, None] * frame_table[None], axis=1)
    flips = jnp.sum(onehot[:, :, None] * flip_table[None], axis=1) * swap_flags[:, None].astype(
        jnp.float32
    )
    residues = residue_types.shape[0]
    shaped = true_frames.reshape(12, residues, 8)
    resolved = jnp.where(flips[None] > 0.5, shaped * sign_table[:, None, None], shaped).reshape(
        12, residues * 8
    )
    rot_pred = pred_frames[:9]
    rot_true = resolved[:9]
    offsets = []
    for column in range(3):
        true_part = (
            rot_true[column] * resolved[9]
            + rot_true[3 + column] * resolved[10]
            + rot_true[6 + column] * resolved[11]
        )
        pred_part = (
            rot_pred[column] * pred_frames[9]
            + rot_pred[3 + column] * pred_frames[10]
            + rot_pred[6 + column] * pred_frames[11]
        )
        offsets.append(true_part - pred_part)
    return (rot_pred, rot_true, jnp.stack(offsets, axis=0), exists.reshape(residues * 8))


def atom_terms(true_atoms, atom_mask, residue_types, swap_flags):
    tables = residue_tables()
    onehot_int = type_onehot(residue_types).astype(jnp.int32)
    onehot = onehot_int.astype(jnp.float32)
    partner_table = jnp.asarray(tables[2], dtype=jnp.int32)
    atom_table = jnp.asarray(tables[0], dtype=jnp.float32)
    partners = jnp.sum(onehot_int[:, :, None] * partner_table[None], axis=1)
    own_slots = jnp.broadcast_to(jnp.arange(14, dtype=jnp.int32)[None, :], partners.shape)
    source = jnp.where(swap_flags[:, None] == 1, partners, own_slots)
    residues = residue_types.shape[0]
    shaped = true_atoms.reshape(3, residues, 14)
    resolved = jnp.take_along_axis(
        shaped, jnp.broadcast_to(source[None], shaped.shape), axis=2
    ).reshape(3, residues * 14)
    mask_resolved = jnp.take_along_axis(atom_mask.reshape(residues, 14), source, axis=1)
    exists = jnp.sum(onehot[:, :, None] * atom_table[None], axis=1)
    weight = (exists * mask_resolved.astype(jnp.float32)).reshape(residues * 14)
    return (resolved, weight)


def clamped_errors(frame_side, atom_side):
    rot_pred, rot_true, offset = frame_side
    pred_pos, true_pos = atom_side
    squares = jnp.zeros((offset.shape[1], pred_pos.shape[1]), jnp.float32)
    for column in range(3):
        error = offset[column][:, None]
        for axis_row in range(3):
            error = error + rot_pred[3 * axis_row + column][:, None] * pred_pos[axis_row][None, :]
            error = error - rot_true[3 * axis_row + column][:, None] * true_pos[axis_row][None, :]
        squares = squares + error * error
    return jnp.minimum(jnp.sqrt(squares + eps_square), clamp_length) / clamp_length


def block_groups(shard_count, shard_cols, pair_limit):
    groups = max(1, min(shard_count, pair_limit // shard_cols))
    while shard_count % groups:
        groups -= 1
    lane_step = 128 // math.gcd(shard_cols, 128)
    return groups


def pair_folder(frame_side, row_exists, shard_cols):
    frame_rows = row_exists.shape[0]
    pair_limit = max(shard_cols, (1 << 20) // frame_rows)

    def add_pairs(carry, pieces, start):
        length = pieces[0].shape[1]
        block_width = length
        shard_count = length // shard_cols
        block_width = block_groups(shard_count, shard_cols, pair_limit) * shard_cols
        turn_count = length // block_width

        def one_block(turn_index, running):
            frame_raw, atom_sum = running
            begin_at = turn_index * block_width
            pred_block = lax.dynamic_slice_in_dim(pieces[0], begin_at, block_width, 1)
            true_block = lax.dynamic_slice_in_dim(pieces[1], begin_at, block_width, 1)
            weight_block = lax.dynamic_slice_in_dim(pieces[2], begin_at, block_width, 1)
            clamped = clamped_errors(frame_side, (pred_block, true_block))
            frame_raw = frame_raw + jnp.sum(clamped * weight_block, axis=1)
            column_sums = jnp.sum(clamped * row_exists[:, None], axis=0)
            atom_sum = lax.dynamic_update_slice_in_dim(atom_sum, column_sums, begin_at, 0)
            return (frame_raw, atom_sum)

        return lax.fori_loop(0, turn_count, one_block, carry)

    return add_pairs


def shards(pred_frames, true_frames, pred_atoms, true_atoms, atom_mask, residue_types, swap_flags):
    rot_pred, rot_true, offset, exists = frame_terms(
        pred_frames, true_frames, residue_types, swap_flags
    )
    true_resolved, weight = atom_terms(true_atoms, atom_mask, residue_types, swap_flags)
    shard_cols = pred_atoms.shape[1]
    rows = side_by_side((rot_pred, rot_true, offset, exists[None, :]), GY, 1, 0)
    row_exists = rows[3][0]
    folder = pair_folder((rows[0], rows[1], rows[2]), row_exists, shard_cols)
    start_state = (
        jnp.zeros(row_exists.shape, jnp.float32),
        jnp.zeros((shard_cols * lax.axis_size(GX),), jnp.float32),
    )
    row_raw, column_sum = folder(
        start_state,
        gather_turned((pred_atoms, true_resolved, weight[None, :]), GX, (1, 1, 1)),
        jnp.int32(0),
    )
    frame_raw = sent_and_summed(row_raw, GY, 0)
    atom_part = sent_and_summed(column_sum, GX, 0)
    frame_sum = exists * frame_raw
    loss_sum, frame_count, atom_count = (
        by_axis(jnp.sum(frame_sum), GX_GY),
        by_axis(jnp.sum(exists), GX_GY),
        by_axis(jnp.sum(weight), GX_GY),
    )
    frame_loss = frame_sum / atom_count
    atom_loss = weight * atom_part / frame_count
    total_loss = (loss_sum / (frame_count * atom_count)).reshape(1)
    return (frame_loss, atom_loss, total_loss)


def solution(mesh):
    finer = Mesh(
        mesh.devices.reshape(mesh.shape["sa"], 8, 2, 4, 2), ("sa", "gx_0", "gx_1", "gy_0", "gy_1")
    )
    placed = (
        P(None, SA_GX_GY),
        P(None, SA_GX_GY),
        P(None, SA_GX_GY),
        P(None, SA_GX_GY),
        P(SA_GX_GY),
        P(SA_GX_GY),
        P(SA_GX_GY),
    )
    return jax.shard_map(
        shards,
        mesh=finer,
        in_specs=placed,
        out_specs=(P(SA_GX_GY), P(SA_GX_GY), P("sa")),
        check_vma=False,
    )
```

profile of v0, /device:TPU:2, one launch (start us, length us, event | category | flops | bytes accessed | tf_op | source)
XLA Modules:
  0.0 205.6 jit_solution(11149782708440451952)
XLA Ops:
  0.6 0.7 broadcast_compare_fusion.2
  1.3 0.7 convert_element_type.45
  2.0 0.8 fusion.10
  2.7 1.0 multiply_reduce_fusion.4
  4.3 0.6 multiply_reduce_fusion.5
  5.6 0.2 copy-done
  5.8 0.1 concatenate.6
  5.9 33.8 %all_gather.6 = f32[22,1024]{1,0:T(8,128)S(1)} all-gather(f32[22,128]{1,0:T(8,128)S(1)} %concatenate.6), channel_id=1, replica_groups=mesh['sa'=2,'gx_0'=8,'gx_1'=2,'gy_0'=4,'gy_1'=2] {'gy_0','gy_1'}, dimensions={1}, use_global_device_ids=true | all-gather | bytes 101376 | tf_op jit(solution)/shard_map/all_gather | solution.py:21
  40.1 0.3 copy-done.7
  40.9 0.1 multiply_reduce_fusion.3
  41.6 0.1 reshape.532
  41.7 9.4 %gather_fusion = f32[672]{0:T(1024)S(1)} fusion(f32[3,16,14]{2,1,0:T(8,128)S(1)} %reshape.529, s32[672]{0:T(1024)S(1)} %reshape.532), kind=kCustom, calls=%fused_computation | custom fusion | bytes 13440 | tf_op jit(solution)/shard_map/jit(take_along_axis)/gather | solution.py:127
  51.2 1.9 gather_fusion.1
  53.2 18.7 %all-gather = f32[16,224,7]{1,2,0:T(8,128)S(1)} all-gather(f32[1,224,7]{1,2,0:T(8,128)S(1)} %maximum_bitcast_fusion), channel_id=1, replica_groups=mesh['sa'=2,'gx_0'=8,'gx_1'=2,'gy_0'=4,'gy_1'=2] {'gx_0','gx_1'}, dimensions={0}, use_global_device_ids=true | all-gather | bytes 106624 | tf_op jit(solution)/shard_map/all_gather | solution.py:28
  71.9 0.1 reshape.548
  72.1 70.5 %while.16 = (s32[]{:T(128)}, f32[1024]{0:T(1024)}, f32[3584]{0:T(1024)S(1)}, f32[3,1024]{1,0:T(4,128)S(1)}, f32[9,1024]{1,0:T(8,128)S(1)}, /*index=5*/f32[3,3584...) while((s32[]{:T(128)}, f32[1024]{0:T(1024)}, ...), condition=%wide.region_7.8_spmd.clone, body=%wide.region_4.7_spmd.clone.sunk | while | flops 82577416 | bytes 480513 | solution.py:180
  72.2 0.1 dynamic-slice_reduce_fusion.7
  72.4 8.3 %multiply_reduce_fusion.15 = f32[896]{0:T(1024)S(1)} fusion(f32[1024]{0:T(1024)S(1)} %bitcast.147, f32[1024]{0:T(1024)S(1)} %bitcast.125, f32[1024]{0:T(1024)S(1)} %bitcast.107, f32[1024]{0:T(1024)S(1)} %bitcast.127, f32[1024]{0:T(1024)S(1)} %bitcast.109, f32[1024]{0:T(1024)S(1)} %bitcast.129, f32[1024]{0:T(1024)S(1)} %bitcast.111, ...), kind=kLoop, calls=%fused_computation.2.clone.1 | loop fusion | flops 41286784 | bytes 115200 | tf_op jit(solution)/shard_map/while/body/eval_jaxpr/reduce_sum | solution.py:176
  80.7 7.8 %multiply_reduce_fusion.14 = f32[1024]{0:T(1024)S(1)} fusion(f32[896]{0:T(1024)S(1)} %multiply_reduce_fusion.13, f32[1024]{0:T(1024)S(1)} %bitcast.126, f32[1024]{0:T(1024)S(1)} %bitcast.108, f32[1024]{0:T(1024)S(1)} %bitcast.128, f32[1024]{0:T(1024)S(1)} %bitcast.110, f32[1024]{0:T(1024)S(1)} %bitcast.130, f32[1024]{0:T(1024)S(1)} %bitcast.112, ...), kind=kLoop, calls=%fused_computation.3.clone.1 | loop fusion | flops 41286656 | bytes 115200 | tf_op jit(solution)/shard_map/while/body/eval_jaxpr/reduce_sum | solution.py:175
  88.5 0.6 select_add_fusion.2
  89.1 0.2 dynamic_update_slice.9
  89.3 0.1 dynamic-slice_reduce_fusion.7
  89.5 8.3 %multiply_reduce_fusion.15 = f32[896]{0:T(1024)S(1)} fusion(f32[1024]{0:T(1024)S(1)} %bitcast.147, f32[1024]{0:T(1024)S(1)} %bitcast.125, f32[1024]{0:T(1024)S(1)} %bitcast.107, f32[1024]{0:T(1024)S(1)} %bitcast.127, f32[1024]{0:T(1024)S(1)} %bitcast.109, f32[1024]{0:T(1024)S(1)} %bitcast.129, f32[1024]{0:T(1024)S(1)} %bitcast.111, ...), kind=kLoop, calls=%fused_computation.2.clone.1 | loop fusion | flops 41286784 | bytes 115200 | tf_op jit(solution)/shard_map/while/body/eval_jaxpr/reduce_sum | solution.py:176
  97.8 7.8 %multiply_reduce_fusion.14 = f32[1024]{0:T(1024)S(1)} fusion(f32[896]{0:T(1024)S(1)} %multiply_reduce_fusion.13, f32[1024]{0:T(1024)S(1)} %bitcast.126, f32[1024]{0:T(1024)S(1)} %bitcast.108, f32[1024]{0:T(1024)S(1)} %bitcast.128, f32[1024]{0:T(1024)S(1)} %bitcast.110, f32[1024]{0:T(1024)S(1)} %bitcast.130, f32[1024]{0:T(1024)S(1)} %bitcast.112, ...), kind=kLoop, calls=%fused_computation.3.clone.1 | loop fusion | flops 41286656 | bytes 115200 | tf_op jit(solution)/shard_map/while/body/eval_jaxpr/reduce_sum | solution.py:175
  105.6 1.3 select_add_fusion.2
  106.9 0.2 dynamic_update_slice.9
  107.1 0.1 dynamic-slice_reduce_fusion.7
  107.3 8.3 %multiply_reduce_fusion.15 = f32[896]{0:T(1024)S(1)} fusion(f32[1024]{0:T(1024)S(1)} %bitcast.147, f32[1024]{0:T(1024)S(1)} %bitcast.125, f32[1024]{0:T(1024)S(1)} %bitcast.107, f32[1024]{0:T(1024)S(1)} %bitcast.127, f32[1024]{0:T(1024)S(1)} %bitcast.109, f32[1024]{0:T(1024)S(1)} %bitcast.129, f32[1024]{0:T(1024)S(1)} %bitcast.111, ...), kind=kLoop, calls=%fused_computation.2.clone.1 | loop fusion | flops 41286784 | bytes 115200 | tf_op jit(solution)/shard_map/while/body/eval_jaxpr/reduce_sum | solution.py:176
  115.5 7.8 %multiply_reduce_fusion.14 = f32[1024]{0:T(1024)S(1)} fusion(f32[896]{0:T(1024)S(1)} %multiply_reduce_fusion.13, f32[1024]{0:T(1024)S(1)} %bitcast.126, f32[1024]{0:T(1024)S(1)} %bitcast.108, f32[1024]{0:T(1024)S(1)} %bitcast.128, f32[1024]{0:T(1024)S(1)} %bitcast.110, f32[1024]{0:T(1024)S(1)} %bitcast.130, f32[1024]{0:T(1024)S(1)} %bitcast.112, ...), kind=kLoop, calls=%fused_computation.3.clone.1 | loop fusion | flops 41286656 | bytes 115200 | tf_op jit(solution)/shard_map/while/body/eval_jaxpr/reduce_sum | solution.py:175
  123.4 1.3 select_add_fusion.2
  124.6 0.2 dynamic_update_slice.9
  124.8 0.1 dynamic-slice_reduce_fusion.7
  125.1 8.3 %multiply_reduce_fusion.15 = f32[896]{0:T(1024)S(1)} fusion(f32[1024]{0:T(1024)S(1)} %bitcast.147, f32[1024]{0:T(1024)S(1)} %bitcast.125, f32[1024]{0:T(1024)S(1)} %bitcast.107, f32[1024]{0:T(1024)S(1)} %bitcast.127, f32[1024]{0:T(1024)S(1)} %bitcast.109, f32[1024]{0:T(1024)S(1)} %bitcast.129, f32[1024]{0:T(1024)S(1)} %bitcast.111, ...), kind=kLoop, calls=%fused_computation.2.clone.1 | loop fusion | flops 41286784 | bytes 115200 | tf_op jit(solution)/shard_map/while/body/eval_jaxpr/reduce_sum | solution.py:176
  133.3 7.8 %multiply_reduce_fusion.14 = f32[1024]{0:T(1024)S(1)} fusion(f32[896]{0:T(1024)S(1)} %multiply_reduce_fusion.13, f32[1024]{0:T(1024)S(1)} %bitcast.126, f32[1024]{0:T(1024)S(1)} %bitcast.108, f32[1024]{0:T(1024)S(1)} %bitcast.128, f32[1024]{0:T(1024)S(1)} %bitcast.110, f32[1024]{0:T(1024)S(1)} %bitcast.130, f32[1024]{0:T(1024)S(1)} %bitcast.112, ...), kind=kLoop, calls=%fused_computation.3.clone.1 | loop fusion | flops 41286656 | bytes 115200 | tf_op jit(solution)/shard_map/while/body/eval_jaxpr/reduce_sum | solution.py:175
  141.2 1.3 select_add_fusion.2
  142.4 0.2 dynamic_update_slice.9
  142.6 9.2 %all-to-all-start = ((f32[8,1,128]{2,1,0:T(1,128)}), f32[8,1,128]{2,1,0:T(1,128)S(1)}, u32[]{:S(2)}, u32[]{:S(2)}) async-start(f32[8,1,128]{2,1,0:T(1,128)} %bitcast.8), calls=%async_computation | async-start | bytes 8192 | tf_op jit(solution)/shard_map/all_to_all | solution.py:44
  152.0 0.6 multiply_reduce_fusion.8
  153.0 0.7 all_to_all.14
  153.7 4.2 %all-to-all-done = f32[8,1,128]{2,1,0:T(1,128)S(1)} async-done(((f32[8,1,128]{2,1,0:T(1,128)}), f32[8,1,128]{2,1,0:T(1,128)S(1)}, u32[]{:S(2)}, u32[]{:S(2)}) %all-to-all-start) | async-done | bytes 4128 | tf_op jit(solution)/shard_map/all_to_all | solution.py:44
  157.9 3.7 %all-to-all-start.1 = ((f32[16,1,224]{2,1,0:T(1,128)}), f32[16,1,224]{2,1,0:T(1,128)S(1)}, u32[]{:S(2)}, u32[]{:S(2)}) async-start(f32[16,1,224]{2,1,0:T(1,128)} %all_to_all.14), calls=%async_computation.1 | async-start | bytes 32768 | tf_op jit(solution)/shard_map/all_to_all | solution.py:44
  161.7 0.6 multiply_reduce_fusion.9
  162.3 17.9 %all-reduce = (f32[]{:T(128)}, f32[]{:T(128)}, f32[]{:T(128)}) all-reduce(f32[]{:T(128)} %multiply_reduce_fusion.8, f32[]{:T(128)} %get-tuple-element.214, f32[]{:T(128)} %multiply_reduce_fusion.9), channel_id=1, replica_groups=mesh['sa'=2,'gx_0'=8,'gx_1'=2,'gy_0'=4,'gy_1'=2] {'gx_0'}, use_global_device_ids=true, to_apply=%region_10.11 | all-reduce | flops 3 | bytes 24 | tf_op jit(solution)/shard_map/psum | solution.py:49
  180.2 3.1 %all-reduce.3 = (f32[]{:T(128)}, f32[]{:T(128)}, f32[]{:T(128)}) all-reduce(f32[]{:T(128)} %get-tuple-element.237, f32[]{:T(128)} %get-tuple-element.238, f32[]{:T(128)} %get-tuple-element.239), channel_id=1, replica_groups=mesh['sa'=2,'gx_0'=8,'gx_1'=2,'gy_0'=4,'gy_1'=2] {'gx_1'}, use_global_device_ids=true, to_apply=%region_11.12 | all-reduce | flops 3 | bytes 24 | tf_op jit(solution)/shard_map/psum | solution.py:49
  183.3 10.0 %all-reduce.1 = (f32[]{:T(128)}, f32[]{:T(128)}, f32[]{:T(128)}) all-reduce(f32[]{:T(128)} %get-tuple-element.246, f32[]{:T(128)} %get-tuple-element.247, f32[]{:T(128)} %get-tuple-element.248), channel_id=1, replica_groups=mesh['sa'=2,'gx_0'=8,'gx_1'=2,'gy_0'=4,'gy_1'=2] {'gy_0'}, use_global_device_ids=true, to_apply=%region_12.13 | all-reduce | flops 3 | bytes 24 | tf_op jit(solution)/shard_map/psum | solution.py:49
  193.2 7.1 %all-reduce.2 = (f32[]{:T(128)}, f32[]{:T(128)}, f32[]{:T(128)}) all-reduce(f32[]{:T(128)} %get-tuple-element.240, f32[]{:T(128)} %get-tuple-element.241, f32[]{:T(128)} %get-tuple-element.242), channel_id=1, replica_groups=mesh['sa'=2,'gx_0'=8,'gx_1'=2,'gy_0'=4,'gy_1'=2] {'gy_1'}, use_global_device_ids=true, to_apply=%region_13.14 | all-reduce | flops 3 | bytes 24 | tf_op jit(solution)/shard_map/psum | solution.py:49
  200.3 1.2 broadcast_divide_fusion
  203.4 1.1 fusion.16
  (90 shorter events, 3.6 us)
Async XLA Ops:
  0.6 3.5 %copy-start.2 = (f32[12,128]{1,0:T(8,128)S(1)}, f32[12,128]{1,0:T(8,128)}, u32[]{:S(2)}) copy-start(f32[12,128]{1,0:T(8,128)} %param.15) | copy-start | bytes 18436
  2.0 2.3 %copy-start.5 = (f32[20,8]{0,1:T(8,128)S(1)}, f32[20,8]{0,1:T(8,128)}, u32[]{:S(2)}) copy-start(f32[20,8]{0,1:T(8,128)} %constant.99.clone) | copy-start | bytes 1924
  2.0 2.3 %copy-start.6 = (f32[20,8]{0,1:T(8,128)S(1)}, f32[20,8]{0,1:T(8,128)}, u32[]{:S(2)}) copy-start(f32[20,8]{0,1:T(8,128)} %constant.98.clone) | copy-start | bytes 1924
  3.7 1.2 copy-start.8
  5.1 0.7 copy-start
  39.7 0.7 copy-start.7
  39.7 1.1 copy-start.3
  39.8 1.2 copy-start.1
  51.2 2.0 copy-start.4
  142.6 15.3 %all-to-all-start = ((f32[8,1,128]{2,1,0:T(1,128)}), f32[8,1,128]{2,1,0:T(1,128)S(1)}, u32[]{:S(2)}, u32[]{:S(2)}) async-start(f32[8,1,128]{2,1,0:T(1,128)} %bitcast.8), calls=%async_computation | async-start | bytes 8192 | tf_op jit(solution)/shard_map/all_to_all | solution.py:44
  157.9 45.4 %all-to-all-start.1 = ((f32[16,1,224]{2,1,0:T(1,128)}), f32[16,1,224]{2,1,0:T(1,128)S(1)}, u32[]{:S(2)}, u32[]{:S(2)}) async-start(f32[16,1,224]{2,1,0:T(1,128)} %all_to_all.14), calls=%async_computation.1 | async-start | bytes 32768 | tf_op jit(solution)/shard_map/all_to_all | solution.py:44
where the time goes:
time: 206 us
  blocking collectives  90.5 us (44%)
  other arithmetic  76.6 us (37%)
  local copies, waits for them, and re-layouts  17.1 us (8%)
  starting transfers between devices  13 us (6%)
  waiting for transfers between devices  4.23 us (2%)
  between operations  4.01 us (2%)
    psum x4, blocking collectives, by_axis(): return functools.reduce(lax.psum, axes, value)  38 us
    all_gather x1, blocking collectives, side_by_side(): result = lax.all_gather(both, axis, axis=dim, tiled=True)  33.8 us
    reduce_sum x4, other arithmetic, one_block(): column_sums = jnp.sum(clamped * row_exists[:, None], axis=0)  33 us
    reduce_sum x4, other arithmetic, one_block(): frame_raw = frame_raw + jnp.sum(clamped * weight_block, axis=1)  31.3 us
    all_gather x1, blocking collectives, gather_turned(): lax.all_gather(both, axis, axis=0, tiled=True)  18.7 us
    all_to_all x2, starting transfers between devices, sent_and_summed(): lax.all_to_all(tiles, axis, split_axis=0, concat_axis=0, tiled=True)  13 us
    gather x3, local copies, waits for them, and re-layouts, atom_terms(): jnp.take_along_axis(shaped, jnp.broadcast_to(source[None], shaped.shape),...  9.56 us
    add x4, other arithmetic, one_block(): frame_raw = frame_raw + jnp.sum(clamped * weight_block, axis=1)  4.41 us
  transfers between devices with their start and end apart: 2, of which 1 were waited for; matrix products, arithmetic and copies ran while one was open for 1% of the time, Pallas kernels for 0%

commit v1 on v0

--- a/solution.py
+++ b/solution.py
@@ -25,7 +25,13 @@
 def gather_turned(arrays, axis, dims):
     turned = [jnp.moveaxis(a, dim, 0) for a, dim in zip(arrays, dims)]
     both = jnp.concatenate([t.reshape(len(t), -1) for t in turned], axis=1)
-    result, at, gathered = (lax.all_gather(both, axis, axis=0, tiled=True), 0, [])
+    result, at, gathered = (
+        jnp.concatenate(
+            lax.all_to_all(jnp.stack([both] * lax.axis_size(axis)), axis, 0, 0), axis=0
+        ),
+        0,
+        [],
+    )
     for t, dim in zip(turned, dims):
         piece = result[:, at : at + t[0].size].reshape(-1, *t.shape[1:])
         gathered.append(jnp.moveaxis(piece, 0, dim))

time: 206 us -> 198 us (0.961)
  blocking collectives: 90.5 us -> 70.2 us
  starting transfers between devices: 13 us -> 25.2 us
    all_gather x1 -> x0, blocking collectives: 18.7 us -> none  [gather_turned(): lax.all_gather(both, axis, axis=0, tiled=True)]
    all_to_all x0 -> x1, starting transfers between devices: none -> 8.71 us  [gather_turned(): lax.all_to_all(jnp.stack([both] * lax.axis_size(axis)), axis, 0, 0)]
    all_to_all x2, starting transfers between devices: 13 us -> 16.5 us  [sent_and_summed(): lax.all_to_all(tiles, axis, split_axis=0, concat_axis=0, tiled=True)]
  transfers between devices with their start and end apart: 2 -> 3, of which waited for: 1 -> 1; matrix products, arithmetic and copies ran while one was open for 1% -> 2% of each run, Pallas kernels for 0% -> 0%
where the time goes in v1:
time: 198 us; the launch traced here: 197 us
  other arithmetic  75.7 us (38%)
  blocking collectives  70.2 us (35%)
  starting transfers between devices  25.2 us (13%)
  local copies, waits for them, and re-layouts  17.5 us (9%)
  waiting for transfers between devices  4.41 us (2%)
  between operations  4.06 us (2%)
    psum x4, blocking collectives, by_axis(): return functools.reduce(lax.psum, axes, value)  38 us
    reduce_sum x4, other arithmetic, one_block(): column_sums = jnp.sum(clamped * row_exists[:, None], axis=0)  32.8 us
    all_gather x1, blocking collectives, side_by_side(): result = lax.all_gather(both, axis, axis=dim, tiled=True)  32.2 us
    reduce_sum x4, other arithmetic, one_block(): frame_raw = frame_raw + jnp.sum(clamped * weight_block, axis=1)  31.3 us
    all_to_all x2, starting transfers between devices, sent_and_summed(): lax.all_to_all(tiles, axis, split_axis=0, concat_axis=0, tiled=True)  16.5 us
    gather x3, local copies, waits for them, and re-layouts, atom_terms(): jnp.take_along_axis(shaped, jnp.broadcast_to(source[None], shaped.shape),...  9.56 us
    all_to_all x1, starting transfers between devices, gather_turned(): lax.all_to_all(jnp.stack([both] * lax.axis_size(axis)), axis, 0, 0)  8.71 us
    all_to_all x2, waiting for transfers between devices, sent_and_summed(): lax.all_to_all(tiles, axis, split_axis=0, concat_axis=0, tiled=True)  4.41 us
  transfers between devices with their start and end apart: 3, of which 1 were waited for; matrix products, arithmetic and copies ran while one was open for 2% of the time, Pallas kernels for 0%

profile of v1, /device:TPU:2, one launch (start us, length us, event | category | flops | bytes accessed | tf_op | source)
XLA Modules:
  0.0 197.1 jit_solution(9959082825866582214)
XLA Ops:
  0.7 0.7 fusion.10
  1.4 1.0 multiply_reduce_fusion.4
  2.7 0.7 broadcast_compare_fusion.2
  4.4 0.1 multiply_reduce_fusion.3
  5.0 0.1 reshape.538
  5.1 9.4 %gather_fusion = f32[672]{0:T(1024)S(1)} fusion(f32[3,16,14]{2,1,0:T(8,128)S(1)} %reshape.534, s32[672]{0:T(1024)S(1)} %reshape.538), kind=kCustom, calls=%fused_computation | custom fusion | bytes 13440 | tf_op jit(solution)/shard_map/jit(take_along_axis)/gather | solution.py:133
  14.6 1.9 gather_fusion.1
  16.6 0.6 stack.2
  17.3 8.7 %all-to-all-start = ((f32[16,224,7]{1,2,0:T(8,128)}), f32[16,224,7]{1,2,0:T(8,128)S(1)}, u32[]{:S(2)}, u32[]{:S(2)}) async-start(f32[16,224,7]{1,2,0:T(8,128)} %stack.2), calls=%async_computation | async-start | bytes 262144 | tf_op jit(solution)/shard_map/all_to_all | solution.py:30
  26.2 0.6 multiply_reduce_fusion.5
  27.2 0.1 slice.335
  27.5 0.2 copy-done
  27.8 0.1 concatenate.6
  27.9 32.2 %all_gather.3 = f32[22,1024]{1,0:T(8,128)S(1)} all-gather(f32[22,128]{1,0:T(8,128)S(1)} %concatenate.6), channel_id=1, replica_groups=mesh['sa'=2,'gx_0'=8,'gx_1'=2,'gy_0'=4,'gy_1'=2] {'gy_0','gy_1'}, dimensions={1}, use_global_device_ids=true | all-gather | bytes 101376 | tf_op jit(solution)/shard_map/all_gather | solution.py:21
  60.2 0.1 reshape.536
  60.4 70.2 %while.16 = (s32[]{:T(128)}, f32[1024]{0:T(1024)}, f32[3584]{0:T(1024)S(1)}, f32[3,1024]{1,0:T(4,128)S(1)}, f32[9,1024]{1,0:T(8,128)S(1)}, /*index=5*/f32[3,3584...) while((s32[]{:T(128)}, f32[1024]{0:T(1024)}, ...), condition=%wide.region_7.8_spmd.clone, body=%wide.region_4.7_spmd.clone.sunk | while | flops 82577416 | bytes 480513 | solution.py:186
  60.5 0.1 dynamic-slice_reduce_fusion.7
  60.7 8.2 %multiply_reduce_fusion.15 = f32[896]{0:T(1024)S(1)} fusion(f32[1024]{0:T(1024)S(1)} %bitcast.145, f32[1024]{0:T(1024)S(1)} %bitcast.123, f32[1024]{0:T(1024)S(1)} %bitcast.105, f32[1024]{0:T(1024)S(1)} %bitcast.125, f32[1024]{0:T(1024)S(1)} %bitcast.107, f32[1024]{0:T(1024)S(1)} %bitcast.127, f32[1024]{0:T(1024)S(1)} %bitcast.109, ...), kind=kLoop, calls=%fused_computation.2.clone.1 | loop fusion | flops 41286784 | bytes 115200 | tf_op jit(solution)/shard_map/while/body/eval_jaxpr/reduce_sum | solution.py:182
  68.9 7.8 %multiply_reduce_fusion.14 = f32[1024]{0:T(1024)S(1)} fusion(f32[896]{0:T(1024)S(1)} %multiply_reduce_fusion.13, f32[1024]{0:T(1024)S(1)} %bitcast.124, f32[1024]{0:T(1024)S(1)} %bitcast.106, f32[1024]{0:T(1024)S(1)} %bitcast.126, f32[1024]{0:T(1024)S(1)} %bitcast.108, f32[1024]{0:T(1024)S(1)} %bitcast.128, f32[1024]{0:T(1024)S(1)} %bitcast.110, ...), kind=kLoop, calls=%fused_computation.3.clone.1 | loop fusion | flops 41286656 | bytes 115200 | tf_op jit(solution)/shard_map/while/body/eval_jaxpr/reduce_sum | solution.py:181
  76.7 0.6 select_add_fusion.2
  77.3 0.2 dynamic_update_slice.9
  77.5 0.1 dynamic-slice_reduce_fusion.7
  77.7 8.2 %multiply_reduce_fusion.15 = f32[896]{0:T(1024)S(1)} fusion(f32[1024]{0:T(1024)S(1)} %bitcast.145, f32[1024]{0:T(1024)S(1)} %bitcast.123, f32[1024]{0:T(1024)S(1)} %bitcast.105, f32[1024]{0:T(1024)S(1)} %bitcast.125, f32[1024]{0:T(1024)S(1)} %bitcast.107, f32[1024]{0:T(1024)S(1)} %bitcast.127, f32[1024]{0:T(1024)S(1)} %bitcast.109, ...), kind=kLoop, calls=%fused_computation.2.clone.1 | loop fusion | flops 41286784 | bytes 115200 | tf_op jit(solution)/shard_map/while/body/eval_jaxpr/reduce_sum | solution.py:182
  85.9 7.8 %multiply_reduce_fusion.14 = f32[1024]{0:T(1024)S(1)} fusion(f32[896]{0:T(1024)S(1)} %multiply_reduce_fusion.13, f32[1024]{0:T(1024)S(1)} %bitcast.124, f32[1024]{0:T(1024)S(1)} %bitcast.106, f32[1024]{0:T(1024)S(1)} %bitcast.126, f32[1024]{0:T(1024)S(1)} %bitcast.108, f32[1024]{0:T(1024)S(1)} %bitcast.128, f32[1024]{0:T(1024)S(1)} %bitcast.110, ...), kind=kLoop, calls=%fused_computation.3.clone.1 | loop fusion | flops 41286656 | bytes 115200 | tf_op jit(solution)/shard_map/while/body/eval_jaxpr/reduce_sum | solution.py:181
  93.8 1.3 select_add_fusion.2
  95.0 0.2 dynamic_update_slice.9
  95.2 0.1 dynamic-slice_reduce_fusion.7
  95.5 8.2 %multiply_reduce_fusion.15 = f32[896]{0:T(1024)S(1)} fusion(f32[1024]{0:T(1024)S(1)} %bitcast.145, f32[1024]{0:T(1024)S(1)} %bitcast.123, f32[1024]{0:T(1024)S(1)} %bitcast.105, f32[1024]{0:T(1024)S(1)} %bitcast.125, f32[1024]{0:T(1024)S(1)} %bitcast.107, f32[1024]{0:T(1024)S(1)} %bitcast.127, f32[1024]{0:T(1024)S(1)} %bitcast.109, ...), kind=kLoop, calls=%fused_computation.2.clone.1 | loop fusion | flops 41286784 | bytes 115200 | tf_op jit(solution)/shard_map/while/body/eval_jaxpr/reduce_sum | solution.py:182
  103.7 7.8 %multiply_reduce_fusion.14 = f32[1024]{0:T(1024)S(1)} fusion(f32[896]{0:T(1024)S(1)} %multiply_reduce_fusion.13, f32[1024]{0:T(1024)S(1)} %bitcast.124, f32[1024]{0:T(1024)S(1)} %bitcast.106, f32[1024]{0:T(1024)S(1)} %bitcast.126, f32[1024]{0:T(1024)S(1)} %bitcast.108, f32[1024]{0:T(1024)S(1)} %bitcast.128, f32[1024]{0:T(1024)S(1)} %bitcast.110, ...), kind=kLoop, calls=%fused_computation.3.clone.1 | loop fusion | flops 41286656 | bytes 115200 | tf_op jit(solution)/shard_map/while/body/eval_jaxpr/reduce_sum | solution.py:181
  111.5 1.3 select_add_fusion.2
  112.8 0.2 dynamic_update_slice.9
  112.9 0.1 dynamic-slice_reduce_fusion.7
  113.2 8.2 %multiply_reduce_fusion.15 = f32[896]{0:T(1024)S(1)} fusion(f32[1024]{0:T(1024)S(1)} %bitcast.145, f32[1024]{0:T(1024)S(1)} %bitcast.123, f32[1024]{0:T(1024)S(1)} %bitcast.105, f32[1024]{0:T(1024)S(1)} %bitcast.125, f32[1024]{0:T(1024)S(1)} %bitcast.107, f32[1024]{0:T(1024)S(1)} %bitcast.127, f32[1024]{0:T(1024)S(1)} %bitcast.109, ...), kind=kLoop, calls=%fused_computation.2.clone.1 | loop fusion | flops 41286784 | bytes 115200 | tf_op jit(solution)/shard_map/while/body/eval_jaxpr/reduce_sum | solution.py:182
  121.4 7.8 %multiply_reduce_fusion.14 = f32[1024]{0:T(1024)S(1)} fusion(f32[896]{0:T(1024)S(1)} %multiply_reduce_fusion.13, f32[1024]{0:T(1024)S(1)} %bitcast.124, f32[1024]{0:T(1024)S(1)} %bitcast.106, f32[1024]{0:T(1024)S(1)} %bitcast.126, f32[1024]{0:T(1024)S(1)} %bitcast.108, f32[1024]{0:T(1024)S(1)} %bitcast.128, f32[1024]{0:T(1024)S(1)} %bitcast.110, ...), kind=kLoop, calls=%fused_computation.3.clone.1 | loop fusion | flops 41286656 | bytes 115200 | tf_op jit(solution)/shard_map/while/body/eval_jaxpr/reduce_sum | solution.py:181
  129.2 1.3 select_add_fusion.2
  130.5 0.2 dynamic_update_slice.9
  130.6 9.2 %all-to-all-start.1 = ((f32[8,1,128]{2,1,0:T(1,128)}), f32[8,1,128]{2,1,0:T(1,128)S(1)}, u32[]{:S(2)}, u32[]{:S(2)}) async-start(f32[8,1,128]{2,1,0:T(1,128)} %bitcast.7), calls=%async_computation.1 | async-start | bytes 8192 | tf_op jit(solution)/shard_map/all_to_all | solution.py:50
  139.9 0.6 multiply_reduce_fusion.8
  140.9 0.7 all_to_all.18
  141.5 4.4 %all-to-all-done.1 = f32[8,1,128]{2,1,0:T(1,128)S(1)} async-done(((f32[8,1,128]{2,1,0:T(1,128)}), f32[8,1,128]{2,1,0:T(1,128)S(1)}, u32[]{:S(2)}, u32[]{:S(2)}) %all-to-all-start.1) | async-done | bytes 4128 | tf_op jit(solution)/shard_map/all_to_all | solution.py:50
  145.9 7.2 %all-to-all-start.2 = ((f32[16,1,224]{2,1,0:T(1,128)}), f32[16,1,224]{2,1,0:T(1,128)S(1)}, u32[]{:S(2)}, u32[]{:S(2)}) async-start(f32[16,1,224]{2,1,0:T(1,128)} %all_to_all.18), calls=%async_computation.2 | async-start | bytes 32768 | tf_op jit(solution)/shard_map/all_to_all | solution.py:50
  153.2 0.6 multiply_reduce_fusion.9
  153.8 17.9 %all-reduce = (f32[]{:T(128)}, f32[]{:T(128)}, f32[]{:T(128)}) all-reduce(f32[]{:T(128)} %multiply_reduce_fusion.8, f32[]{:T(128)} %get-tuple-element.214, f32[]{:T(128)} %multiply_reduce_fusion.9), channel_id=1, replica_groups=mesh['sa'=2,'gx_0'=8,'gx_1'=2,'gy_0'=4,'gy_1'=2] {'gx_0'}, use_global_device_ids=true, to_apply=%region_10.11 | all-reduce | flops 3 | bytes 24 | tf_op jit(solution)/shard_map/psum | solution.py:55
  171.7 3.1 %all-reduce.3 = (f32[]{:T(128)}, f32[]{:T(128)}, f32[]{:T(128)}) all-reduce(f32[]{:T(128)} %get-tuple-element.237, f32[]{:T(128)} %get-tuple-element.238, f32[]{:T(128)} %get-tuple-element.239), channel_id=1, replica_groups=mesh['sa'=2,'gx_0'=8,'gx_1'=2,'gy_0'=4,'gy_1'=2] {'gx_1'}, use_global_device_ids=true, to_apply=%region_11.12 | all-reduce | flops 3 | bytes 24 | tf_op jit(solution)/shard_map/psum | solution.py:55
  174.8 10.0 %all-reduce.1 = (f32[]{:T(128)}, f32[]{:T(128)}, f32[]{:T(128)}) all-reduce(f32[]{:T(128)} %get-tuple-element.246, f32[]{:T(128)} %get-tuple-element.247, f32[]{:T(128)} %get-tuple-element.248), channel_id=1, replica_groups=mesh['sa'=2,'gx_0'=8,'gx_1'=2,'gy_0'=4,'gy_1'=2] {'gy_0'}, use_global_device_ids=true, to_apply=%region_12.13 | all-reduce | flops 3 | bytes 24 | tf_op jit(solution)/shard_map/psum | solution.py:55
  184.7 7.1 %all-reduce.2 = (f32[]{:T(128)}, f32[]{:T(128)}, f32[]{:T(128)}) all-reduce(f32[]{:T(128)} %get-tuple-element.240, f32[]{:T(128)} %get-tuple-element.241, f32[]{:T(128)} %get-tuple-element.242), channel_id=1, replica_groups=mesh['sa'=2,'gx_0'=8,'gx_1'=2,'gy_0'=4,'gy_1'=2] {'gy_1'}, use_global_device_ids=true, to_apply=%region_13.14 | all-reduce | flops 3 | bytes 24 | tf_op jit(solution)/shard_map/psum | solution.py:55
  191.8 1.2 broadcast_divide_fusion
  194.9 1.1 fusion.16
  (94 shorter events, 3.5 us)
Async XLA Ops:
  0.6 3.7 %copy-start.1 = (f32[20,14]{0,1:T(8,128)S(1)}, f32[20,14]{0,1:T(8,128)}, u32[]{:S(2)}) copy-start(f32[20,14]{0,1:T(8,128)} %constant.102.clone) | copy-start | bytes 3364
  0.6 3.2 %copy-start.7 = (s32[224]{0:T(256)S(1)}, s32[224]{0:T(256)}, u32[]{:S(2)}) copy-start(s32[224]{0:T(256)} %param.18) | copy-start | bytes 2692
  0.7 3.6 %copy-start.3 = (f32[3,224]{1,0:T(4,128)S(1)}, f32[3,224]{1,0:T(4,128)}, u32[]{:S(2)}) copy-start(f32[3,224]{1,0:T(4,128)} %param.17) | copy-start | bytes 8068
  14.6 2.0 %copy-start.4 = (f32[3,224]{1,0:T(4,128)S(1)}, f32[3,224]{1,0:T(4,128)}, u32[]{:S(2)}) copy-start(f32[3,224]{1,0:T(4,128)} %param.16) | copy-start | bytes 8068
  17.2 8.7 %copy-start.9 = (s32[16]{0:T(128)S(1)}, s32[16]{0:T(128)}, u32[]{:S(2)}) copy-start(s32[16]{0:T(128)} %param.20) | copy-start | bytes 196
  17.2 8.9 %copy-start.2 = (f32[12,128]{1,0:T(8,128)S(1)}, f32[12,128]{1,0:T(8,128)}, u32[]{:S(2)}) copy-start(f32[12,128]{1,0:T(8,128)} %param.15) | copy-start | bytes 18436
  17.3 9.0 %copy-start.5 = (f32[20,8]{0,1:T(8,128)S(1)}, f32[20,8]{0,1:T(8,128)}, u32[]{:S(2)}) copy-start(f32[20,8]{0,1:T(8,128)} %constant.99.clone) | copy-start | bytes 1924
  17.3 9.0 %copy-start.6 = (f32[20,8]{0,1:T(8,128)S(1)}, f32[20,8]{0,1:T(8,128)}, u32[]{:S(2)}) copy-start(f32[20,8]{0,1:T(8,128)} %constant.98.clone) | copy-start | bytes 1924
  17.3 42.9 %all-to-all-start = ((f32[16,224,7]{1,2,0:T(8,128)}), f32[16,224,7]{1,2,0:T(8,128)S(1)}, u32[]{:S(2)}, u32[]{:S(2)}) async-start(f32[16,224,7]{1,2,0:T(8,128)} %stack.2), calls=%async_computation | async-start | bytes 262144 | tf_op jit(solution)/shard_map/all_to_all | solution.py:30
  26.0 1.0 copy-start.8
  27.0 0.7 copy-start
  130.6 15.3 %all-to-all-start.1 = ((f32[8,1,128]{2,1,0:T(1,128)}), f32[8,1,128]{2,1,0:T(1,128)S(1)}, u32[]{:S(2)}, u32[]{:S(2)}) async-start(f32[8,1,128]{2,1,0:T(1,128)} %bitcast.7), calls=%async_computation.1 | async-start | bytes 8192 | tf_op jit(solution)/shard_map/all_to_all | solution.py:50
  145.9 48.9 %all-to-all-start.2 = ((f32[16,1,224]{2,1,0:T(1,128)}), f32[16,1,224]{2,1,0:T(1,128)S(1)}, u32[]{:S(2)}, u32[]{:S(2)}) async-start(f32[16,1,224]{2,1,0:T(1,128)} %all_to_all.18), calls=%async_computation.2 | async-start | bytes 32768 | tf_op jit(solution)/shard_map/all_to_all | solution.py:50
